TPU v7x, 512 devices: a whole 4x4x16 slice. The times are simulated.
512 devices in a mesh: lat: 16 (over z_hi, y), lon: 32 (over z_lo, x, core).
Axes of the slice: x: 4, y: 4, z: 16 (z_hi: 4, z_lo: 4; z = z_hi * 4 + z_lo), core: 2. Of those that a mesh axis runs over, the one named last changes fastest.
Arguments:
- queries: float32 [64, 1024, 512], P('lat', 'lon'), may hold values from -80 to 80
- key_rows: float32 [512, 512], P(('lat', 'lon')), may hold values from -8 to 8
- value_rows: float32 [512, 512], P(('lat', 'lon')), may hold values from -6 to 6
- cotangent: float32 [64, 1024, 512], P('lat', 'lon'), may hold values from -25 to 25
- conv_taps: float32 [9, 512], replicated, may hold values from -1.75 to 1.75
Outputs:
- query_grad: float32 [64, 1024, 512], P('lat', 'lon')
- key_grad: float32 [512, 512], P(('lat', 'lon'))
- value_grad: float32 [512, 512], P(('lat', 'lon'))
- tap_update: float32 [9, 512], replicated
All inputs are finite; a program needn't handle non-finite values.
Results may differ from a plain program's by a relative error of at most 0.0003.
Values sent between devices are 32-bit elements; how exact they have to be, the bound alone decides.
A program may use at most 64 MiB of HBM per device.

v0:
```python
import jax
import jax.numpy as jnp
from jax import lax
from jax.sharding import PartitionSpec as P

HD = 64
HIGH = lax.Precision.HIGHEST
OFFSETS = ((-1, -1), (-1, 0), (-1, 1), (0, -1), (0, 0), (0, 1), (1, -1), (1, 0), (1, 1))


def joined_along(pieces, dim):
    lengths = list(pieces.shape[1:])
    lengths[dim] *= pieces.shape[0]
    return jnp.moveaxis(pieces, 0, dim).reshape(lengths)


def copy_for_each(value, axis):
    copies = jnp.broadcast_to(value, (lax.axis_size(axis), *value.shape))
    return lax.all_to_all(copies, axis, split_axis=0, concat_axis=0, tiled=True)


def gather_directly(value, axis, dim):
    return joined_along(copy_for_each(value, axis), dim)


def extended(value, sides, width):
    for axis, dim in sides:
        peers, length = (lax.axis_size(axis), value.shape[dim])
        up = [(i, (i + 1) % peers) for i in range(peers)]
        down = [(j, i) for i, j in up]
        last = lax.slice_in_dim(value, length - width, length, axis=dim)
        initial = lax.slice_in_dim(value, 0, width, axis=dim)
        before = lax.ppermute(last, axis, up)
        after = lax.ppermute(initial, axis, down)
        value = jnp.concatenate([before, value, after], axis=dim)
    return value


def cut_along(value, dim, peers):
    lengths = value.shape
    pieces = value.reshape(*lengths[:dim], peers, lengths[dim] // peers, *lengths[dim + 1 :])
    return jnp.moveaxis(pieces, dim, 0)


def summed_on_arrival(value, axis, dim):
    peers = lax.axis_size(axis)
    pieces = lax.all_to_all(cut_along(value, dim, peers), axis, 0, 0, tiled=True)
    return jnp.sum(pieces, axis=0)


def split_heads(matrix):
    return matrix.reshape(matrix.shape[0], -1, HD)


def latitude_weights(row_count, band_index, band_count):
    line_total = row_count * band_count
    centres = (jnp.arange(line_total, dtype=jnp.float32) + 0.5) * (jnp.pi / line_total)
    mean_cosine = jnp.sum(jnp.sin(centres)) / line_total
    mine = (band_index * row_count + jnp.arange(row_count, dtype=jnp.int32)).astype(jnp.float32)
    return jnp.sin((mine + 0.5) * (jnp.pi / line_total)) / mean_cosine


def close_poles(padded, row_dim, band_index, band_count):
    height = padded.shape[row_dim]
    positions = jnp.arange(height)
    outside = (positions == 0) & (band_index == 0) | (positions == height - 1) & (
        band_index == band_count - 1
    )
    shape_mask = [1] * padded.ndim
    shape_mask[row_dim] = height
    return jnp.where(outside.reshape(shape_mask), 0.0, padded)


def spread_taps(weighted, grad_padded, conv_taps):
    row_count, col_count = (weighted.shape[0], weighted.shape[1])
    result = weighted
    for tap_index, (shift_row, shift_col) in enumerate(OFFSETS):
        result = (
            result
            + conv_taps[tap_index]
            * grad_padded[
                1 - shift_row : 1 - shift_row + row_count, 1 - shift_col : 1 - shift_col + col_count
            ]
        )
    return result


def tap_terms(weighted, out_padded):
    row_count, col_count = (weighted.shape[0], weighted.shape[1])
    term_list = []
    for shift_row, shift_col in OFFSETS:
        term_list.append(
            jnp.sum(
                out_padded[
                    1 + shift_row : 1 + shift_row + row_count,
                    1 + shift_col : 1 + shift_col + col_count,
                ]
                * weighted,
                axis=(0, 1),
            )
        )
    return jnp.stack(term_list)


def group_logits(query_part, key_part):
    return jnp.einsum(
        "qhd,khd->hqk", split_heads(query_part), split_heads(key_part), precision=HIGH
    ) * HD ** (-0.5)


def body(queries, key_rows, value_rows, cotangent, conv_taps):
    row_count, col_count, channels = queries.shape
    band_count = lax.axis_size("lat")
    band_index = lax.axis_index("lat")
    weighted = cotangent * latitude_weights(row_count, band_index, band_count)[:, None, None]
    paired_rows = jnp.concatenate([key_rows, value_rows], 1)
    paired_sector = gather_directly(paired_rows, "lon", 0)
    paired_all = lax.all_gather(paired_sector, "lat", axis=0, tiled=True)
    key_all = paired_all[:, :channels]
    value_all = paired_all[:, channels:]
    token_count = row_count * col_count
    key_count = key_all.shape[0]
    query_flat = queries.reshape(token_count, channels)
    group_width = 2 * HD
    group_count = channels // group_width
    outputs = []
    peaks = []
    sums_soft = []
    for group_index in range(group_count):
        col_start = group_index * group_width
        col_stop = col_start + group_width
        logits = group_logits(query_flat[:, col_start:col_stop], key_all[:, col_start:col_stop])
        row_peak = jnp.max(logits, -1, keepdims=True)
        raised = jnp.exp(logits - row_peak)
        normaliser = jnp.sum(raised, -1, keepdims=True)
        soft_weights = raised / normaliser
        outputs.append(
            jnp.einsum(
                "hqk,khd->qhd",
                soft_weights,
                split_heads(value_all[:, col_start:col_stop]),
                precision=HIGH,
            ).reshape(token_count, group_width)
        )
        peaks.append(row_peak)
        sums_soft.append(normaliser)
    out_flat = jnp.concatenate(outputs, 1)
    out_grid = out_flat.reshape(row_count, col_count, channels)
    both_padded = close_poles(
        extended(jnp.stack([weighted, out_grid]), (("lat", 1), ("lon", 2)), 1),
        1,
        band_index,
        band_count,
    )
    grad_padded = both_padded[0]
    out_padded = both_padded[1]
    out_grad = spread_taps(weighted, grad_padded, conv_taps)
    tap_sum = lax.psum(tap_terms(weighted, out_padded), ("lat", "lon"))
    tap_update = tap_sum / jnp.sqrt(jnp.mean(tap_sum * tap_sum) + 1e-06)
    grad_flat = out_grad.reshape(token_count, channels)
    query_parts = []
    key_parts = []
    value_parts = []
    for group_index in range(group_count):
        col_start = group_index * group_width
        col_stop = col_start + group_width
        query_heads = split_heads(query_flat[:, col_start:col_stop])
        key_heads = split_heads(key_all[:, col_start:col_stop])
        logits = jnp.einsum("qhd,khd->hqk", query_heads, key_heads, precision=HIGH) * HD ** (-0.5)
        soft_weights = jnp.exp(logits - peaks[group_index]) / sums_soft[group_index]
        grad_heads = split_heads(grad_flat[:, col_start:col_stop])
        value_parts.append(
            jnp.einsum("hqk,qhd->khd", soft_weights, grad_heads, precision=HIGH).reshape(
                key_count, group_width
            )
        )
        prob_grad = jnp.einsum(
            "qhd,khd->hqk",
            grad_heads,
            split_heads(value_all[:, col_start:col_stop]),
            precision=HIGH,
        )
        row_dot = jnp.transpose(
            jnp.sum(grad_heads * split_heads(out_flat[:, col_start:col_stop]), -1)
        )[:, :, None]
        logit_grad = soft_weights * (prob_grad - row_dot)
        query_parts.append(
            (
                jnp.einsum("hqk,khd->qhd", logit_grad, key_heads, precision=HIGH) * HD ** (-0.5)
            ).reshape(token_count, group_width)
        )
        key_parts.append(
            (
                jnp.einsum("hqk,qhd->khd", logit_grad, query_heads, precision=HIGH) * HD ** (-0.5)
            ).reshape(key_count, group_width)
        )
    paired_terms = jnp.concatenate(key_parts + value_parts, 1)
    paired_band = lax.psum_scatter(paired_terms, "lat", scatter_dimension=0, tiled=True)
    paired_grad = summed_on_arrival(paired_band, "lon", 0)
    key_grad = paired_grad[:, :channels]
    value_grad = paired_grad[:, channels:]
    query_grad = jnp.concatenate(query_parts, 1).reshape(row_count, col_count, channels)
    return (query_grad, key_grad, value_grad, tap_update)


def solution(mesh):
    placed = (
        P("lat", "lon", None),
        P(("lat", "lon"), None),
        P(("lat", "lon"), None),
        P("lat", "lon", None),
        P(),
    )
    return jax.shard_map(
        body,
        mesh=mesh,
        in_specs=placed,
        out_specs=(P("lat", "lon", None), P(("lat", "lon"), None), P(("lat", "lon"), None), P()),
        check_vma=False,
    )
```

profile of v0, /device:TPU:1, one launch (start us, length us, event | category | flops | bytes accessed | tf_op | source)
XLA Modules:
  0.0 343.2 jit_solution(12765066276765064027)
XLA Ops:
  7.2 0.7 pad_maximum_fusion.13
  8.0 18.8 %all_to_all.10 = f32[32,1,1024]{2,1,0:T(1,128)} all-to-all(f32[32,1,1024]{2,1,0:T(1,128)S(1)} %broadcast_in_dim.10), channel_id=1, replica_groups=mesh['lat'=16,'lon'=32] {'lon'}, dimensions={0} | all-to-all | bytes 262144 | tf_op jit(solution)/shard_map/all_to_all | solution.py:19
  26.9 1.0 fusion.53
  27.9 0.7 copy.151
  28.6 0.7 copy.150
  30.8 1.0 fusion.50
  31.8 88.1 %all-gather.3.cloned.1.call-done = f32[512,1,1024]{2,1,0:T(1,128)} async-done(((f32[32,1,1024]{2,1,0:T(1,128)}), f32[512,1,1024]{2,1,0:T(1,128)}) %all-gather.3.cloned.1.call-update) | async-done | bytes 2097168 | tf_op jit(solution)/shard_map/all_gather | solution.py:118
  120.0 2.1 copy.158
  122.8 0.8 copy.91
  123.9 0.9 copy.83
  124.8 1.0 fusion.56
  126.7 1.0 fusion.58
  127.8 1.1 convolution_bitcast_fusion.2
  128.9 1.0 copy.90
  130.0 1.0 fusion.57
  131.9 1.0 fusion.59
  133.1 1.4 convolution_bitcast_fusion.3
  134.8 2.1 collective-permute-start
  136.9 9.2 %collective-permute-start.1 = (f32[2,1,32,512]{3,2,1,0:T(8,128)S(1)}, f32[2,1,32,512]{3,2,1,0:T(8,128)S(1)}, u32[]{:S(2)}, u32[]{:S(2)}) collective-permute-start(f32[2,1,32,512]{3,2,1,0:T(8,128)S(1)} %get-tuple-element.26), channel_id=1, source_target_pairs={{32,0},{64,32},{96,64},{128,96},{160,128},{192,160},{224,192},{256... | collective-permute-start | bytes 393224 | tf_op jit(solution)/shard_map/ppermute | solution.py:34
  146.1 4.7 %collective-permute-done = f32[2,1,32,512]{3,2,1,0:T(8,128)S(1)} collective-permute-done((f32[2,1,32,512]{3,2,1,0:T(8,128)S(1)}, f32[2,1,32,512]{3,2,1,0:T(8,128)S(1)}, u32[]{:S(2)}, u32[]{:S(2)}) %collective-permute-start) | collective-permute-done | bytes 131104 | tf_op jit(solution)/shard_map/ppermute | solution.py:33
  150.9 3.2 collective-permute-start.2
  154.1 2.1 collective-permute-start.3
  156.3 3.3 collective-permute-done.3
  160.2 0.7 fusion.52
  160.9 1.6 copy.153
  162.4 0.9 multiply_reduce_fusion.3
  163.3 1.6 copy.155
  164.9 0.9 multiply_reduce_fusion.1
  165.8 1.6 copy.154
  167.3 0.9 multiply_reduce_fusion.2
  168.2 1.6 copy.156
  169.8 0.9 multiply_reduce_fusion
  170.8 1.6 fusion.38
  172.4 1.0 fusion
  174.9 1.0 fusion.2
  175.9 0.7 convolution_multiply_fusion.6
  177.4 1.0 fusion.1
  178.4 0.7 convolution_multiply_fusion.5
  179.9 1.0 fusion.3
  180.9 0.7 convolution_multiply_fusion.7
  181.8 1.9 copy.146
  184.1 117.4 %psum.7 = f32[9,512]{1,0:T(8,128)S(1)} all-reduce(f32[9,512]{1,0:T(8,128)S(1)} %stack.47), channel_id=1, replica_groups=mesh['lat'=16,'lon'=32] {'lat','lon'}, use_global_device_ids=true, to_apply=%region_24.25 | all-reduce | flops 4608 | bytes 36864 | tf_op jit(solution)/shard_map/psum | solution.py:158
  304.9 13.6 %reduce-scatter.4.cloned.1.call-done = f32[32,1024]{1,0:T(8,128)} async-done(((f32[512,1024]{1,0:T(8,128)}), f32[32,1024]{1,0:T(8,128)}) %reduce-scatter.4.cloned.1.call-update) | async-done | bytes 131088
  318.5 1.1 copy.147
  319.6 0.8 copy.125
  320.4 6.7 %all-to-all-start.1 = ((f32[32,1,1024]{2,1,0:T(1,128)}), f32[32,1,1024]{2,1,0:T(1,128)S(1)}, u32[]{:S(2)}, u32[]{:S(2)}) async-start(f32[32,1,1024]{2,1,0:T(1,128)} %copy.125), calls=%async_computation.1 | async-start | bytes 262144 | tf_op jit(solution)/shard_map/all_to_all | solution.py:47
  327.8 0.7 pad_maximum_fusion
  329.2 6.5 %all-to-all-done.1 = f32[32,1,1024]{2,1,0:T(1,128)S(1)} async-done(((f32[32,1,1024]{2,1,0:T(1,128)}), f32[32,1,1024]{2,1,0:T(1,128)S(1)}, u32[]{:S(2)}, u32[]{:S(2)}) %all-to-all-start.1) | async-done | bytes 131104 | tf_op jit(solution)/shard_map/all_to_all | solution.py:47
  (138 shorter events, 13.0 us)
Async XLA Ops:
  7.2 112.8 %all-gather.3.cloned.1.call-start = ((), (), s32[]{:S(2)}) async-start(), calls=%async_computation.3 | async-start | bytes 2228224 | tf_op jit(solution)/shard_map/all_gather | solution.py:118
  26.8 291.7 %reduce-scatter.4.cloned.1.call-start = ((), (), s32[]{:S(2)}) async-start(), calls=%async_computation.4 | async-start | bytes 2228224
  29.4 95.3 %copy-start.17 = (f32[128,128]{0,1:T(8,128)}, f32[128,128]{0,1:T(8,128)S(1)}, u32[]{:S(2)}) copy-start(f32[128,128]{0,1:T(8,128)S(1)} %copy.152) | copy-start | bytes 196612
  122.5 3.4 copy-start.1
  122.6 3.8 %copy-start.28 = (f32[512,128]{0,1:T(8,128)}, f32[512,128]{0,1:T(8,128)S(1)}, u32[]{:S(2)}) copy-start(f32[512,128]{0,1:T(8,128)S(1)} %copy.96) | copy-start | bytes 786436
  123.8 2.9 copy-start.3
  123.9 3.9 %copy-start.26 = (f32[512,128]{0,1:T(8,128)}, f32[512,128]{0,1:T(8,128)S(1)}, u32[]{:S(2)}) copy-start(f32[512,128]{0,1:T(8,128)S(1)} %copy.86) | copy-start | bytes 786436
  123.9 2.8 copy-start.15
  126.4 3.6 %copy-start.19 = (f32[128,2,64]{0,2,1:T(8,128)}, f32[128,2,64]{0,2,1:T(8,128)S(1)}, u32[]{:S(2)}) copy-start(f32[128,2,64]{0,2,1:T(8,128)S(1)} %convolution_bitcast_fusion) | copy-start | bytes 196612
  126.4 3.6 %copy-start.13 = (f32[128,128]{0,1:T(8,128)S(1)}, f32[128,128]{0,1:T(8,128)}, u32[]{:S(2)}) copy-start(f32[128,128]{0,1:T(8,128)} %copy.151) | copy-start | bytes 196612
  127.7 3.4 %copy-start.24 = (f32[512,128]{0,1:T(8,128)S(1)}, f32[512,128]{0,1:T(8,128)}, u32[]{:S(2)}) copy-start(f32[512,128]{0,1:T(8,128)} %copy.91) | copy-start | bytes 786436
  131.7 19.2 %copy-start.21 = (f32[128,2,64]{0,2,1:T(8,128)}, f32[128,2,64]{0,2,1:T(8,128)S(1)}, u32[]{:S(2)}) copy-start(f32[128,2,64]{0,2,1:T(8,128)S(1)} %convolution_bitcast_fusion.1) | copy-start | bytes 196612
  132.9 13.2 %copy-start.34 = (f32[9,512]{1,0:T(8,128)S(1)}, f32[9,512]{1,0:T(8,128)}, u32[]{:S(2)}) copy-start(f32[9,512]{1,0:T(8,128)} %param.9) | copy-start | bytes 55300
  134.5 16.3 %copy-start.22 = (f32[128,2,64]{0,2,1:T(8,128)}, f32[128,2,64]{0,2,1:T(8,128)S(1)}, u32[]{:S(2)}) copy-start(f32[128,2,64]{0,2,1:T(8,128)S(1)} %convolution_bitcast_fusion.3) | copy-start | bytes 196612
  134.8 16.0 %collective-permute-start = (f32[2,1,32,512]{3,2,1,0:T(8,128)S(1)}, f32[2,1,32,512]{3,2,1,0:T(8,128)S(1)}, u32[]{:S(2)}, u32[]{:S(2)}) collective-permute-start(f32[2,1,32,512]{3,2,1,0:T(8,128)S(1)} %get-tuple-element.25), channel_id=1, source_target_pairs={{0,32},{32,64},{64,96},{96,128},{128,160},{160,192},{192,224},{224... | collective-permute-start | bytes 393224 | tf_op jit(solution)/shard_map/ppermute | solution.py:33
  136.9 13.9 %collective-permute-start.1 = (f32[2,1,32,512]{3,2,1,0:T(8,128)S(1)}, f32[2,1,32,512]{3,2,1,0:T(8,128)S(1)}, u32[]{:S(2)}, u32[]{:S(2)}) collective-permute-start(f32[2,1,32,512]{3,2,1,0:T(8,128)S(1)} %get-tuple-element.26), channel_id=1, source_target_pairs={{32,0},{64,32},{96,64},{128,96},{160,128},{192,160},{224,192},{256... | collective-permute-start | bytes 393224 | tf_op jit(solution)/shard_map/ppermute | solution.py:34
  150.9 9.0 %copy-start = (f32[4,32,512]{2,1,0:T(8,128)S(1)}, f32[4,32,512]{2,1,0:T(8,128)}, u32[]{:S(2)}) copy-start(f32[4,32,512]{2,1,0:T(8,128)} %param.8) | copy-start | bytes 786436
  150.9 5.4 %collective-permute-start.2 = (f32[2,6,1,512]{3,2,1,0:T(1,128)S(1)}, f32[2,6,1,512]{3,2,1,0:T(1,128)S(1)}, u32[]{:S(2)}, u32[]{:S(2)}) collective-permute-start(f32[2,6,1,512]{3,2,1,0:T(1,128)S(1)} %get-tuple-element.23), channel_id=1, source_target_pairs={{0,1},{1,2},{2,3},{3,4},{4,5},{5,6},{6,7},{7,8},{8,9},{9,10},{10,1... | collective-permute-start | bytes 73736 | tf_op jit(solution)/shard_map/ppermute | solution.py:33
  154.1 5.4 %collective-permute-start.3 = (f32[2,6,1,512]{3,2,1,0:T(1,128)S(1)}, f32[2,6,1,512]{3,2,1,0:T(1,128)S(1)}, u32[]{:S(2)}, u32[]{:S(2)}) collective-permute-start(f32[2,6,1,512]{3,2,1,0:T(1,128)S(1)} %get-tuple-element.24), channel_id=1, source_target_pairs={{1,0},{2,1},{3,2},{4,3},{5,4},{6,5},{7,6},{8,7},{9,8},{10,9},{11,1... | collective-permute-start | bytes 73736 | tf_op jit(solution)/shard_map/ppermute | solution.py:34
  159.9 9.9 %copy-start.20 = (f32[128,2,64]{0,2,1:T(8,128)S(1)}, f32[128,2,64]{0,2,1:T(8,128)}, u32[]{:S(2)}) copy-start(f32[128,2,64]{0,2,1:T(8,128)} %copy-done.19) | copy-start | bytes 196612
  169.8 2.5 copy-start.29
  169.8 2.5 copy-start.33
  170.7 2.6 copy-start.18
  170.7 3.4 copy-start.32
  172.4 2.5 copy-start.27
  173.4 2.5 copy-start.7
  174.1 1.8 copy-start.16
  174.1 2.5 copy-start.31
  174.8 2.5 copy-start.25
  175.9 2.5 copy-start.9
  176.6 1.8 copy-start.14
  176.6 2.5 copy-start.30
  177.4 2.5 copy-start.23
  178.4 1.4 copy-start.11
  180.9 0.9 copy-start.5
  183.7 119.1 %copy-start.2 = (f32[512,128]{0,1:T(8,128)S(1)}, f32[512,128]{0,1:T(8,128)}, u32[]{:S(2)}) copy-start(f32[512,128]{0,1:T(8,128)} %copy-done.1) | copy-start | bytes 786436
  183.7 119.1 %copy-start.8 = (f32[2,128,512]{1,2,0:T(8,128)S(1)}, f32[2,128,512]{1,2,0:T(8,128)}, u32[]{:S(2)}) copy-start(f32[2,128,512]{1,2,0:T(8,128)} %copy-done.7) | copy-start | bytes 1572868
  183.7 119.8 %copy-start.4 = (f32[512,128]{0,1:T(8,128)S(1)}, f32[512,128]{0,1:T(8,128)}, u32[]{:S(2)}) copy-start(f32[512,128]{0,1:T(8,128)} %copy-done.3) | copy-start | bytes 786436
  183.7 119.8 %copy-start.10 = (f32[2,128,512]{1,2,0:T(8,128)S(1)}, f32[2,128,512]{1,2,0:T(8,128)}, u32[]{:S(2)}) copy-start(f32[2,128,512]{1,2,0:T(8,128)} %copy-done.9) | copy-start | bytes 1572868
  183.7 120.5 %copy-start.12 = (f32[2,128,512]{1,2,0:T(8,128)S(1)}, f32[2,128,512]{1,2,0:T(8,128)}, u32[]{:S(2)}) copy-start(f32[2,128,512]{1,2,0:T(8,128)} %copy-done.11) | copy-start | bytes 1572868
  303.4 23.7 %copy-start.6 = (f32[2,128,512]{1,2,0:T(8,128)S(1)}, f32[2,128,512]{1,2,0:T(8,128)}, u32[]{:S(2)}) copy-start(f32[2,128,512]{1,2,0:T(8,128)} %copy-done.5) | copy-start | bytes 1572868
  320.4 15.2 %all-to-all-start.1 = ((f32[32,1,1024]{2,1,0:T(1,128)}), f32[32,1,1024]{2,1,0:T(1,128)S(1)}, u32[]{:S(2)}, u32[]{:S(2)}) async-start(f32[32,1,1024]{2,1,0:T(1,128)} %copy.125), calls=%async_computation.1 | async-start | bytes 262144 | tf_op jit(solution)/shard_map/all_to_all | solution.py:47
Sparse Core Ops, SparseCore 0:
  26.9 93.0 all-gather.2
  183.8 134.6 reduce-scatter.3
where the time goes:
time: 344 us; the launch traced here: 343 us
  blocking collectives  136 us (40%)
  waiting for transfers between devices  116 us (34%)
  starting transfers between devices  23.4 us (7%)
  local copies, waits for them, and re-layouts  21.9 us (6%)
  matrix products  19.9 us (6%)
  between operations  16.2 us (5%)
  other arithmetic  9.35 us (3%)
    psum x1, blocking collectives, body(): tap_sum = lax.psum(tap_terms(weighted, out_padded), ('lat', 'lon'))  117 us
    all_gather x1, waiting for transfers between devices, body(): paired_all = lax.all_gather(paired_sector, 'lat', axis=0, tiled=True)  88.1 us
    all_to_all x1, blocking collectives, copy_for_each(): return lax.all_to_all(copies, axis, split_axis=0, concat_axis=0, tiled=True)  18.8 us
    unnamed x3, waiting for transfers between devices  13.6 us
    unnamed x88, local copies, waits for them, and re-layouts  13.2 us
    ppermute x2, starting transfers between devices, extended(): after = lax.ppermute(initial, axis, down)  11.3 us
  transfers between devices with their start and end apart: 7, of which 5 were waited for; matrix products, arithmetic and copies ran while one was open for 3% of the time, Pallas kernels for 0%

commit v1 on v0

--- a/solution.py
+++ b/solution.py
@@ -115,7 +115,9 @@
     weighted = cotangent * latitude_weights(row_count, band_index, band_count)[:, None, None]
     paired_rows = jnp.concatenate([key_rows, value_rows], 1)
     paired_sector = gather_directly(paired_rows, "lon", 0)
-    paired_all = lax.all_gather(paired_sector, "lat", axis=0, tiled=True)
+    paired_all = jnp.concatenate(
+        lax.all_to_all(jnp.stack([paired_sector] * lax.axis_size("lat")), "lat", 0, 0), axis=0
+    )
     key_all = paired_all[:, :channels]
     value_all = paired_all[:, channels:]
     token_count = row_count * col_count

time: 344 us -> 359 us (1.044)
  starting transfers between devices: 23.4 us -> 39 us
  blocking collectives: 136 us -> 141 us
  other arithmetic: 9.35 us -> 4.88 us
  local copies, waits for them, and re-layouts: 21.9 us -> 18.3 us
    all_to_all x0 -> x1, waiting for transfers between devices: none -> 93.8 us  [body(): lax.all_to_all(jnp.stack([paired_sector] * lax.axis_size('lat')), 'lat',...]
    all_gather x1 -> x0, waiting for transfers between devices: 88.1 us -> none  [body(): paired_all = lax.all_gather(paired_sector, 'lat', axis=0, tiled=True)]
    all_to_all x0 -> x1, starting transfers between devices: none -> 15 us  [body(): lax.all_to_all(jnp.stack([paired_sector] * lax.axis_size('lat')), 'lat',...]
    unnamed x88 -> x108, local copies, waits for them, and re-layouts: 13.2 us -> 6.39 us
    psum x1, blocking collectives: 117 us -> 123 us  [body(): tap_sum = lax.psum(tap_terms(weighted, out_padded), ('lat', 'lon'))]
    ppermute x2, waiting for transfers between devices: 4.69 us -> 0.81 us  [extended(): before = lax.ppermute(last, axis, up)]
    unnamed x3 -> x2, waiting for transfers between devices: 13.6 us -> 11.9 us
  transfers between devices with their start and end apart: 7 -> 7, of which waited for: 5 -> 6; matrix products, arithmetic and copies ran while one was open for 3% -> 2% of each run, Pallas kernels for 0% -> 0%
where the time goes in v1:
time: 359 us
  blocking collectives  141 us (39%)
  waiting for transfers between devices  117 us (33%)
  starting transfers between devices  39 us (11%)
  matrix products  21.3 us (6%)
  local copies, waits for them, and re-layouts  18.3 us (5%)
  between operations  16.4 us (5%)
  other arithmetic  4.88 us (1%)
    psum x1, blocking collectives, body(): tap_sum = lax.psum(tap_terms(weighted, out_padded), ('lat', 'lon'))  123 us
    all_to_all x1, waiting for transfers between devices, body(): lax.all_to_all(jnp.stack([paired_sector] * lax.axis_size('lat')), 'lat',...  93.8 us
    all_to_all x1, blocking collectives, copy_for_each(): return lax.all_to_all(copies, axis, split_axis=0, concat_axis=0, tiled=True)  18.3 us
    all_to_all x1, starting transfers between devices, body(): lax.all_to_all(jnp.stack([paired_sector] * lax.axis_size('lat')), 'lat',...  15 us
    unnamed x2, waiting for transfers between devices  11.9 us
    ppermute x2, starting transfers between devices, extended(): after = lax.ppermute(initial, axis, down)  11.5 us
  transfers between devices with their start and end apart: 7, of which 6 were waited for; matrix products, arithmetic and copies ran while one was open for 2% of the time, Pallas kernels for 0%

profile of v1, /device:TPU:1, one launch (start us, length us, event | category | flops | bytes accessed | tf_op | source)
XLA Modules:
  0.0 358.7 jit_solution(9468416502977244210)
XLA Ops:
  7.2 0.7 pad_maximum_fusion.13
  7.9 18.3 %all_to_all.15 = f32[32,1,1024]{2,1,0:T(1,128)S(1)} all-to-all(f32[32,1,1024]{2,1,0:T(1,128)S(1)} %broadcast_in_dim.10), channel_id=1, replica_groups=mesh['lat'=16,'lon'=32] {'lon'}, dimensions={0} | all-to-all | bytes 262144 | tf_op jit(solution)/shard_map/all_to_all | solution.py:19
  26.3 1.6 stack.39
  27.9 15.0 %all-to-all-start.1 = ((f32[16,32,1024]{2,1,0:T(8,128)}), f32[16,32,1024]{2,1,0:T(8,128)S(1)}, u32[]{:S(2)}, u32[]{:S(2)}) async-start(f32[16,32,1024]{2,1,0:T(8,128)} %stack.39), calls=%async_computation.1 | async-start | bytes 4194304 | tf_op jit(solution)/shard_map/all_to_all | solution.py:119
  43.4 0.7 sine_reduce_fusion
  44.9 93.8 %all-to-all-done.1 = f32[16,32,1024]{2,1,0:T(8,128)S(1)} async-done(((f32[16,32,1024]{2,1,0:T(8,128)}), f32[16,32,1024]{2,1,0:T(8,128)S(1)}, u32[]{:S(2)}, u32[]{:S(2)}) %all-to-all-start.1) | async-done | bytes 2097184 | tf_op jit(solution)/shard_map/all_to_all | solution.py:119
  138.7 1.3 fusion.51
  139.9 1.2 copy.89
  141.1 1.1 copy.105
  142.2 0.9 copy.104
  143.1 1.1 copy.100
  144.2 0.8 copy.99
  145.5 1.0 fusion.58
  147.4 1.0 fusion.57
  148.5 1.4 convolution_bitcast_fusion.1
  150.2 1.0 fusion.56
  151.4 1.6 convolution_bitcast_fusion
  153.8 1.0 fusion.59
  154.9 0.7 copy-done.7
  156.1 0.6 copy-done.33
  157.0 1.9 collective-permute-start
  158.9 9.4 %collective-permute-start.1 = (f32[2,1,32,512]{3,2,1,0:T(8,128)S(1)}, f32[2,1,32,512]{3,2,1,0:T(8,128)S(1)}, u32[]{:S(2)}, u32[]{:S(2)}) collective-permute-start(f32[2,1,32,512]{3,2,1,0:T(8,128)S(1)} %get-tuple-element.26), channel_id=1, source_target_pairs={{32,0},{64,32},{96,64},{128,96},{160,128},{192,160},{224,192},{256... | collective-permute-start | bytes 393224 | tf_op jit(solution)/shard_map/ppermute | solution.py:34
  168.3 0.8 collective-permute-done
  169.1 1.1 collective-permute-done.1
  170.3 4.4 %collective-permute-start.2 = (f32[2,6,1,512]{3,2,1,0:T(1,128)S(1)}, f32[2,6,1,512]{3,2,1,0:T(1,128)S(1)}, u32[]{:S(2)}, u32[]{:S(2)}) collective-permute-start(f32[2,6,1,512]{3,2,1,0:T(1,128)S(1)} %get-tuple-element.23), channel_id=1, source_target_pairs={{0,1},{1,2},{2,3},{3,4},{4,5},{5,6},{6,7},{7,8},{8,9},{9,10},{10,1... | collective-permute-start | bytes 73736 | tf_op jit(solution)/shard_map/ppermute | solution.py:33
  174.7 2.1 collective-permute-start.3
  176.8 3.3 collective-permute-done.3
  181.8 0.7 fusion.38
  182.5 2.0 fusion
  184.5 0.7 convolution_multiply_fusion.4
  185.2 0.7 fusion.44
  186.0 1.0 fusion.2
  187.0 0.7 convolution_multiply_fusion.6
  187.7 0.7 fusion.41
  188.5 1.9 fusion.1
  190.4 0.7 convolution_multiply_fusion.5
  191.1 0.7 fusion.47
  191.8 1.0 fusion.3
  192.9 0.7 convolution_multiply_fusion.7
  193.9 1.9 copy.154
  196.2 123.1 %psum.7 = f32[9,512]{1,0:T(8,128)S(1)} all-reduce(f32[9,512]{1,0:T(8,128)S(1)} %stack.51), channel_id=1, replica_groups=mesh['lat'=16,'lon'=32] {'lat','lon'}, use_global_device_ids=true, to_apply=%region_24.25 | all-reduce | flops 4608 | bytes 36864 | tf_op jit(solution)/shard_map/psum | solution.py:160
  322.7 11.9 %reduce-scatter.4.cloned.1.call-done = f32[32,1024]{1,0:T(8,128)} async-done(((f32[512,1024]{1,0:T(8,128)}), f32[32,1024]{1,0:T(8,128)}) %reduce-scatter.4.cloned.1.call-update) | async-done | bytes 131088
  334.6 1.1 copy.155
  335.7 0.8 copy.133
  336.5 6.2 %all-to-all-start.2 = ((f32[32,1,1024]{2,1,0:T(1,128)}), f32[32,1,1024]{2,1,0:T(1,128)S(1)}, u32[]{:S(2)}, u32[]{:S(2)}) async-start(f32[32,1,1024]{2,1,0:T(1,128)} %copy.133), calls=%async_computation.2 | async-start | bytes 262144 | tf_op jit(solution)/shard_map/all_to_all | solution.py:47
  343.4 0.7 pad_maximum_fusion
  344.1 0.6 broadcast_divide_fusion
  344.7 6.5 %all-to-all-done.2 = f32[32,1,1024]{2,1,0:T(1,128)S(1)} async-done(((f32[32,1,1024]{2,1,0:T(1,128)}), f32[32,1,1024]{2,1,0:T(1,128)S(1)}, u32[]{:S(2)}, u32[]{:S(2)}) %all-to-all-start.2) | async-done | bytes 131104 | tf_op jit(solution)/shard_map/all_to_all | solution.py:47
  (158 shorter events, 10.3 us)
Async XLA Ops:
  27.9 15.1 %copy-start.35 = (f32[4,32,512]{2,1,0:T(8,128)S(1)}, f32[4,32,512]{2,1,0:T(8,128)}, u32[]{:S(2)}) copy-start(f32[4,32,512]{2,1,0:T(8,128)} %param.5) | copy-start | bytes 786436
  27.9 16.9 %copy-start = (f32[4,32,512]{2,1,0:T(8,128)S(1)}, f32[4,32,512]{2,1,0:T(8,128)}, u32[]{:S(2)}) copy-start(f32[4,32,512]{2,1,0:T(8,128)} %param.8) | copy-start | bytes 786436
  27.9 110.8 %all-to-all-start.1 = ((f32[16,32,1024]{2,1,0:T(8,128)}), f32[16,32,1024]{2,1,0:T(8,128)S(1)}, u32[]{:S(2)}, u32[]{:S(2)}) async-start(f32[16,32,1024]{2,1,0:T(8,128)} %stack.39), calls=%async_computation.1 | async-start | bytes 4194304 | tf_op jit(solution)/shard_map/all_to_all | solution.py:119
  42.9 291.7 %reduce-scatter.4.cloned.1.call-start = ((), (), s32[]{:S(2)}) async-start(), calls=%async_computation.4 | async-start | bytes 2228224
  43.3 102.2 %copy-start.23 = (f32[128,128]{0,1:T(8,128)}, f32[128,128]{0,1:T(8,128)S(1)}, u32[]{:S(2)}) copy-start(f32[128,128]{0,1:T(8,128)S(1)} %copy.158) | copy-start | bytes 196612
  43.4 106.8 %copy-start.25 = (f32[128,128]{0,1:T(8,128)}, f32[128,128]{0,1:T(8,128)S(1)}, u32[]{:S(2)}) copy-start(f32[128,128]{0,1:T(8,128)S(1)} %copy.160) | copy-start | bytes 196612
  139.9 4.2 %copy-start.22 = (f32[512,128]{1,0:T(8,128)S(1)}, f32[512,128]{1,0:T(8,128)}, u32[]{:S(2)}) copy-start(f32[512,128]{1,0:T(8,128)} %get-tuple-element.17) | copy-start | bytes 786436
  139.9 5.1 %copy-start.21 = (f32[512,128]{1,0:T(8,128)S(1)}, f32[512,128]{1,0:T(8,128)}, u32[]{:S(2)}) copy-start(f32[512,128]{1,0:T(8,128)} %get-tuple-element.18) | copy-start | bytes 786436
  139.9 5.2 %copy-start.20 = (f32[512,128]{1,0:T(8,128)S(1)}, f32[512,128]{1,0:T(8,128)}, u32[]{:S(2)}) copy-start(f32[512,128]{1,0:T(8,128)} %get-tuple-element.19) | copy-start | bytes 786436
  139.9 5.4 %copy-start.19 = (f32[512,128]{1,0:T(8,128)S(1)}, f32[512,128]{1,0:T(8,128)}, u32[]{:S(2)}) copy-start(f32[512,128]{1,0:T(8,128)} %get-tuple-element.20) | copy-start | bytes 786436
  142.2 8.0 %copy-start.1 = (f32[512,128]{0,1:T(8,128)}, f32[512,128]{0,1:T(8,128)S(1)}, u32[]{:S(2)}) copy-start(f32[512,128]{0,1:T(8,128)S(1)} %copy.105) | copy-start | bytes 786436
  145.1 2.0 copy-start.3
  145.3 2.1 copy-start.39
  145.5 9.5 %copy-start.36 = (f32[512,128]{0,1:T(8,128)}, f32[512,128]{0,1:T(8,128)S(1)}, u32[]{:S(2)}) copy-start(f32[512,128]{0,1:T(8,128)S(1)} %copy.91) | copy-start | bytes 786436
  146.5 2.0 copy-start.5
  147.1 2.8 copy-start.27
  150.0 3.8 %copy-start.29 = (f32[128,2,64]{0,2,1:T(8,128)}, f32[128,2,64]{0,2,1:T(8,128)S(1)}, u32[]{:S(2)}) copy-start(f32[128,2,64]{0,2,1:T(8,128)S(1)} %convolution_bitcast_fusion.1) | copy-start | bytes 196612
  151.2 3.7 %copy-start.9 = (f32[2,128,512]{1,2,0:T(8,128)}, f32[2,128,512]{1,2,0:T(8,128)S(1)}, u32[]{:S(2)}) copy-start(f32[2,128,512]{1,2,0:T(8,128)S(1)} %get-tuple-element.47) | copy-start | bytes 1572868
  154.8 13.5 %copy-start.44 = (f32[9,512]{1,0:T(8,128)S(1)}, f32[9,512]{1,0:T(8,128)}, u32[]{:S(2)}) copy-start(f32[9,512]{1,0:T(8,128)} %param.9) | copy-start | bytes 55300
  157.0 12.2 %collective-permute-start = (f32[2,1,32,512]{3,2,1,0:T(8,128)S(1)}, f32[2,1,32,512]{3,2,1,0:T(8,128)S(1)}, u32[]{:S(2)}, u32[]{:S(2)}) collective-permute-start(f32[2,1,32,512]{3,2,1,0:T(8,128)S(1)} %get-tuple-element.25), channel_id=1, source_target_pairs={{0,32},{32,64},{64,96},{96,128},{128,160},{160,192},{192,224},{224... | collective-permute-start | bytes 393224 | tf_op jit(solution)/shard_map/ppermute | solution.py:33
  158.9 11.3 %collective-permute-start.1 = (f32[2,1,32,512]{3,2,1,0:T(8,128)S(1)}, f32[2,1,32,512]{3,2,1,0:T(8,128)S(1)}, u32[]{:S(2)}, u32[]{:S(2)}) collective-permute-start(f32[2,1,32,512]{3,2,1,0:T(8,128)S(1)} %get-tuple-element.26), channel_id=1, source_target_pairs={{32,0},{64,32},{96,64},{128,96},{160,128},{192,160},{224,192},{256... | collective-permute-start | bytes 393224 | tf_op jit(solution)/shard_map/ppermute | solution.py:34
  170.3 6.6 %collective-permute-start.2 = (f32[2,6,1,512]{3,2,1,0:T(1,128)S(1)}, f32[2,6,1,512]{3,2,1,0:T(1,128)S(1)}, u32[]{:S(2)}, u32[]{:S(2)}) collective-permute-start(f32[2,6,1,512]{3,2,1,0:T(1,128)S(1)} %get-tuple-element.23), channel_id=1, source_target_pairs={{0,1},{1,2},{2,3},{3,4},{4,5},{5,6},{6,7},{7,8},{8,9},{9,10},{10,1... | collective-permute-start | bytes 73736 | tf_op jit(solution)/shard_map/ppermute | solution.py:33
  174.7 5.4 %collective-permute-start.3 = (f32[2,6,1,512]{3,2,1,0:T(1,128)S(1)}, f32[2,6,1,512]{3,2,1,0:T(1,128)S(1)}, u32[]{:S(2)}, u32[]{:S(2)}) collective-permute-start(f32[2,6,1,512]{3,2,1,0:T(1,128)S(1)} %get-tuple-element.24), channel_id=1, source_target_pairs={{1,0},{2,1},{3,2},{4,3},{5,4},{6,5},{7,6},{8,7},{9,8},{10,9},{11,1... | collective-permute-start | bytes 73736 | tf_op jit(solution)/shard_map/ppermute | solution.py:34
  180.5 0.8 copy-start.34
  180.5 1.0 copy-start.30
  180.5 1.1 copy-start.28
  180.5 1.2 copy-start.32
  180.5 1.2 copy-start.10
  181.3 3.2 copy-start.41
  181.4 6.3 %copy-start.43 = (f32[128,128]{0,1:T(8,128)}, f32[128,128]{0,1:T(8,128)S(1)}, u32[]{:S(2)}) copy-start(f32[128,128]{0,1:T(8,128)S(1)} %copy.163) | copy-start | bytes 196612
  181.7 2.8 copy-start.26
  181.8 3.5 copy-start.6
  182.5 3.5 copy-start.40
  184.5 2.5 copy-start.13
  185.2 1.8 copy-start.24
  186.0 2.5 copy-start.38
  187.0 3.4 copy-start.15
  187.7 3.4 copy-start.8
  187.7 3.4 copy-start.42
  188.5 3.4 copy-start.37
  190.4 2.5 copy-start.17
  195.8 124.9 %copy-start.2 = (f32[512,128]{0,1:T(8,128)S(1)}, f32[512,128]{0,1:T(8,128)}, u32[]{:S(2)}) copy-start(f32[512,128]{0,1:T(8,128)} %copy-done.1) | copy-start | bytes 786436
  195.8 124.9 %copy-start.14 = (f32[2,128,512]{1,2,0:T(8,128)S(1)}, f32[2,128,512]{1,2,0:T(8,128)}, u32[]{:S(2)}) copy-start(f32[2,128,512]{1,2,0:T(8,128)} %copy-done.13) | copy-start | bytes 1572868
  195.8 125.5 %copy-start.4 = (f32[512,128]{0,1:T(8,128)S(1)}, f32[512,128]{0,1:T(8,128)}, u32[]{:S(2)}) copy-start(f32[512,128]{0,1:T(8,128)} %copy-done.3) | copy-start | bytes 786436
  195.8 125.5 %copy-start.16 = (f32[2,128,512]{1,2,0:T(8,128)S(1)}, f32[2,128,512]{1,2,0:T(8,128)}, u32[]{:S(2)}) copy-start(f32[2,128,512]{1,2,0:T(8,128)} %copy-done.15) | copy-start | bytes 1572868
  195.8 126.2 %copy-start.18 = (f32[2,128,512]{1,2,0:T(8,128)S(1)}, f32[2,128,512]{1,2,0:T(8,128)}, u32[]{:S(2)}) copy-start(f32[2,128,512]{1,2,0:T(8,128)} %copy-done.17) | copy-start | bytes 1572868
  321.2 21.5 %copy-start.12 = (f32[2,128,512]{1,2,0:T(8,128)S(1)}, f32[2,128,512]{1,2,0:T(8,128)}, u32[]{:S(2)}) copy-start(f32[2,128,512]{1,2,0:T(8,128)} %copy-done.11) | copy-start | bytes 1572868
  336.5 14.7 %all-to-all-start.2 = ((f32[32,1,1024]{2,1,0:T(1,128)}), f32[32,1,1024]{2,1,0:T(1,128)S(1)}, u32[]{:S(2)}, u32[]{:S(2)}) async-start(f32[32,1,1024]{2,1,0:T(1,128)} %copy.133), calls=%async_computation.2 | async-start | bytes 262144 | tf_op jit(solution)/shard_map/all_to_all | solution.py:47
  (4 other events, 2.8 us)
Sparse Core Ops, SparseCore 0:
  195.9 138.6 reduce-scatter.3
